TPU v7x, 32 devices: a whole 2x2x4 slice. The times are simulated.
32 devices in a mesh: lon: 8 (over z, core), head: 4 (over y, x).
Axes of the slice: x: 2, y: 2, z: 4, core: 2. Of those that a mesh axis runs over, the one named last changes fastest.
Arguments:
- image_tokens: bfloat16 [64, 128, 3072], P(None, 'lon'), may hold values from -6 to 6
- conditioning: bfloat16 [3072], replicated, may hold values from -6 to 6
- mod_weight: bfloat16 [3072, 3, 3072], P(('lon', 'head')), may hold values from -0.21875 to 0.21875
- mod_bias: bfloat16 [3, 3072], replicated, may hold values from -3 to 3
- qkv_weight: bfloat16 [3072, 3, 3072], P('lon', None, 'head'), may hold values from -0.109375 to 0.109375
- qkv_bias: bfloat16 [3, 3072], P(None, 'head'), may hold values from -3 to 3
- q_gain: float32 [128], replicated, may hold values from 0.5 to 12
- k_gain: float32 [128], replicated, may hold values from 0.5 to 12
- text_kv: bfloat16 [2, 512, 3072], P(None, 'lon', 'head'), may hold values from -6 to 6
- proj_weight: bfloat16 [3072, 3072], P('lon', 'head'), may hold values from -0.109375 to 0.109375
- proj_bias: bfloat16 [3072], replicated, may hold values from -3 to 3
Outputs:
- block_output: bfloat16 [64, 128, 3072], P(None, 'lon', 'head')
All inputs are finite; a program needn't handle non-finite values.
Results may differ from a plain program's by a relative error of at most 0.0109.
The roundings to bfloat16 on the way count: a program that leaves them out, or rounds other values in their place, can miss the bound.
Values may be sent and summed in bfloat16 or wider, within the bound.
A program may use at most 128 MiB of HBM per device.

v0:
```python
import math
import jax
import jax.numpy as jnp
from jax import lax
from jax.sharding import PartitionSpec as P

RADIUS = 15
QROWS = 16


def padded_2(cells, sides, width):
    for axis, dim in sides:
        count = lax.axis_size(axis)
        head = lax.slice_in_dim(cells, 0, width, axis=dim)
        tail = lax.slice_in_dim(cells, cells.shape[dim] - width, cells.shape[dim], axis=dim)
        cells = jnp.concatenate(
            [
                lax.ppermute(tail, axis, [(i, (i + 1) % count) for i in range(count)]),
                cells,
                lax.ppermute(head, axis, [((i + 1) % count, i) for i in range(count)]),
            ],
            axis=dim,
        )
    return cells


def rms_scale(entries, gain):
    mean_square = jnp.mean(entries * entries, axis=-1, keepdims=True)
    return entries * lax.rsqrt(mean_square + 1e-06) * gain


def window_mask(row_first, q_rows, q_cols, k_rows, k_cols, lat_total):
    query_index = jnp.arange(q_rows * q_cols, dtype=jnp.int32)
    key_index = jnp.arange(k_rows * k_cols, dtype=jnp.int32)
    query_row = (query_index // q_cols)[:, None]
    query_col = (query_index % q_cols)[:, None]
    key_row = (key_index // k_cols)[None, :]
    key_col = (key_index % k_cols)[None, :]
    global_row = row_first + key_row - RADIUS
    near_rows = jnp.abs(key_row - RADIUS - query_row) <= RADIUS
    near_cols = jnp.abs(key_col - RADIUS - query_col) <= RADIUS
    inside = (global_row >= 0) & (global_row < lat_total)
    return near_rows & near_cols & inside


def attend(queries, key_block, value_block, text_keys, text_values, row_first, lat_total):
    q_rows, q_cols, heads_here, head_dim = queries.shape
    k_rows, k_cols = (key_block.shape[0], key_block.shape[1])
    flat_query = queries.reshape(q_rows * q_cols, heads_here, head_dim)
    flat_keys = key_block.reshape(k_rows * k_cols, heads_here, head_dim)
    flat_values = value_block.reshape(k_rows * k_cols, heads_here, head_dim)
    factor = 1.0 / math.sqrt(head_dim)
    image_scores = (
        jnp.einsum("qhd,khd->hqk", flat_query, flat_keys, preferred_element_type=jnp.float32)
        * factor
    )
    text_scores = (
        jnp.einsum("qhd,khd->hqk", flat_query, text_keys, preferred_element_type=jnp.float32)
        * factor
    )
    allowed = window_mask(row_first, q_rows, q_cols, k_rows, k_cols, lat_total)
    image_scores = jnp.where(allowed[None], image_scores, -jnp.inf)
    highest = jnp.maximum(
        jnp.max(image_scores, axis=2, keepdims=True), jnp.max(text_scores, axis=2, keepdims=True)
    )
    image_exp = jnp.exp(image_scores - highest)
    text_exp = jnp.exp(text_scores - highest)
    normaliser = jnp.sum(image_exp, axis=2, keepdims=True) + jnp.sum(
        text_exp, axis=2, keepdims=True
    )
    image_probs = (image_exp / normaliser).astype(jnp.bfloat16)
    text_probs = (text_exp / normaliser).astype(jnp.bfloat16)
    combined = jnp.einsum(
        "hqk,khd->qhd", image_probs, flat_values, preferred_element_type=jnp.float32
    )
    combined = combined + jnp.einsum(
        "hqk,khd->qhd", text_probs, text_values, preferred_element_type=jnp.float32
    )
    return combined.astype(jnp.bfloat16).reshape(q_rows, q_cols, heads_here * head_dim)


def body(
    image_tokens,
    conditioning,
    mod_weight,
    mod_bias,
    qkv_weight,
    qkv_bias,
    q_gain,
    k_gain,
    text_kv,
    proj_weight,
    proj_bias,
):
    lat_rows, col_count, model_width = image_tokens.shape
    token_count = lat_rows * col_count
    head_groups = lax.axis_size("head")
    slice_rows = mod_weight.shape[0]
    row_offset = (lax.axis_index("lon") * head_groups + lax.axis_index("head")) * slice_rows
    silu_part = jax.nn.silu(
        lax.dynamic_slice_in_dim(conditioning, row_offset, slice_rows, 0).astype(jnp.float32)
    )
    partial_mod = jnp.dot(
        silu_part,
        mod_weight.reshape(slice_rows, 3 * model_width).astype(jnp.float32),
        precision=lax.Precision.HIGHEST,
    )
    modulation = lax.psum(partial_mod, ("lon", "head")).reshape(3, model_width) + mod_bias.astype(
        jnp.float32
    )
    token_values = image_tokens.reshape(token_count, model_width).astype(jnp.float32)
    average = jnp.mean(token_values, axis=1, keepdims=True)
    centred = token_values - average
    variance = jnp.mean(centred * centred, axis=1, keepdims=True)
    modulated = (
        (1.0 + modulation[1]) * (centred * lax.rsqrt(variance + 1e-06)) + modulation[0]
    ).astype(jnp.bfloat16)
    local_inner = qkv_weight.shape[2]
    head_dim = q_gain.shape[0]
    local_heads = local_inner // head_dim
    shard_rows = lax.all_gather(qkv_weight, "lon", axis=0, tiled=True)
    row_total = shard_rows.shape[0]
    projected = jnp.dot(
        modulated,
        shard_rows.reshape(row_total, 3 * local_inner),
        preferred_element_type=jnp.float32,
    )
    projected = projected.reshape(token_count, 3, local_inner) + qkv_bias.astype(jnp.float32)
    queries = rms_scale(
        projected[:, 0].reshape(lat_rows, col_count, local_heads, head_dim), q_gain
    ).astype(jnp.bfloat16)
    keys_normed = rms_scale(
        projected[:, 1].reshape(lat_rows, col_count, local_heads, head_dim), k_gain
    ).astype(jnp.bfloat16)
    values_image = projected[:, 2].astype(jnp.bfloat16).reshape(lat_rows, col_count, local_inner)
    key_value = jnp.stack(
        [keys_normed.reshape(lat_rows, col_count, local_inner), values_image], axis=2
    )
    widened = padded_2(key_value, (("lon", 1),), RADIUS)
    padded = jnp.pad(widened, ((RADIUS, RADIUS), (0, 0), (0, 0), (0, 0)))
    text_panel = lax.all_gather(text_kv, "lon", axis=1, tiled=True)
    text_count = text_panel.shape[1]
    text_keys = text_panel[0].reshape(text_count, local_heads, head_dim)
    text_values = text_panel[1].reshape(text_count, local_heads, head_dim)
    key_cols = col_count + 2 * RADIUS

    def one_block(block_index):
        row_first = block_index * QROWS
        query_block = lax.dynamic_slice_in_dim(queries, row_first, QROWS, 0)
        pair_block = lax.dynamic_slice_in_dim(padded, row_first, QROWS + 2 * RADIUS, 0)
        key_block = pair_block[:, :, 0].reshape(QROWS + 2 * RADIUS, key_cols, local_heads, head_dim)
        value_block = pair_block[:, :, 1].reshape(
            QROWS + 2 * RADIUS, key_cols, local_heads, head_dim
        )
        return attend(
            query_block, key_block, value_block, text_keys, text_values, row_first, lat_rows
        )

    attended = lax.map(one_block, jnp.arange(lat_rows // QROWS, dtype=jnp.int32)).reshape(
        token_count, local_inner
    )
    out_cols = model_width // head_groups
    col_offset = lax.axis_index("head") * out_cols
    proj_columns = lax.all_gather(proj_weight, "lon", axis=0, tiled=True)
    own_rows = lax.all_to_all(proj_columns, "head", split_axis=0, concat_axis=1, tiled=True)
    partial_out = jnp.dot(attended, own_rows, preferred_element_type=jnp.float32)
    out_sum = lax.psum_scatter(partial_out, "head", scatter_dimension=1, tiled=True)
    own_image = lax.dynamic_slice_in_dim(
        image_tokens.reshape(token_count, model_width), col_offset, out_cols, 1
    ).astype(jnp.float32)
    own_gate = lax.dynamic_slice_in_dim(modulation[2], col_offset, out_cols, 0)
    own_bias = lax.dynamic_slice_in_dim(proj_bias, col_offset, out_cols, 0).astype(jnp.float32)
    block_output = (own_image + own_gate * (out_sum + own_bias)).astype(jnp.bfloat16)
    return block_output.reshape(lat_rows, col_count, out_cols)


def solution(mesh):
    placed = (
        P(None, "lon", None),
        P(),
        P(("lon", "head"), None, None),
        P(),
        P("lon", None, "head"),
        P(None, "head"),
        P(),
        P(),
        P(None, "lon", "head"),
        P("lon", "head"),
        P(),
    )
    return jax.shard_map(
        body, mesh=mesh, in_specs=placed, out_specs=P(None, "lon", "head"), check_vma=False
    )
```

profile of v0, /device:TPU:0, one launch (start us, length us, event | category | flops | bytes accessed | tf_op | source)
XLA Modules:
  0.0 694.7 jit_solution(13399464902569084253)
XLA Ops:
  13.9 45.9 %psum.7 = f32[3,3072]{1,0:T(4,128)S(1)} all-reduce(f32[3,3072]{1,0:T(4,128)S(1)} %reshape.296), channel_id=1, replica_groups=mesh['lon'=8,'head'=4] {'lon','head'}, use_global_device_ids=true, to_apply=%region_0.1 | all-reduce | flops 9216 | bytes 73728 | tf_op jit(solution)/shard_map/psum | solution.py:108
  69.9 7.3 %fusion.40 = bf16[64,16,3072]{2,1,0:T(8,128)(2,1)} fusion(bf16[64,16,3072]{2,1,0:T(8,128)(2,1)S(1)} %bitcast.76, f32[3072]{0:T(1024)S(1)} %bitcast.90, f32[64,16]{1,0:T(8,128)S(1)} %add_rsqrt_fusion.2, f32[64,16]{1,0:T(8,128)S(1)} %broadcast_multiply_fusion, f32[3072]{0:T(1024)S(1)} %bitcast.91), kind=kLoop, calls=%fused_computation.68 | loop fusion | flops 18874368 | bytes 12615680 | tf_op jit(solution)/shard_map/convert_element_type | solution.py:117
  77.2 5.0 all-to-all-start
  82.4 112.0 %all-gather.4.cloned.1.call-done = bf16[3072,3,768]{0,2,1:T(8,128)(2,1)} async-done(((bf16[384,3,768]{0,2,1:T(8,128)(2,1)}), bf16[3072,3,768]{0,2,1:T(8,128)(2,1)}) %all-gather.4.cloned.1.call-update) | async-done | bytes 14155792 | tf_op jit(solution)/shard_map/all_gather | solution.py:121
  194.4 19.7 %broadcast_add_fusion.1 = f32[1024,3,768]{2,0,1:T(8,128)S(1)} fusion(f32[3,768]{1,0:T(4,128)S(1)} %convert_element_type.84, bf16[1024,3072,1]{1,0,2:T(8,128)(2,1)} %bitcast.83, bf16[3072,3,768]{0,2,1:T(8,128)(2,1)} %all-gather.4.cloned.1.call-done), kind=kOutput, calls=%fused_computation.69 | convolution fusion | flops 14497873920 | bytes 29893632 | tf_op jit(solution)/shard_map/dot_general | solution.py:123
  248.6 5.6 fusion.52
  268.1 6.7 copy.94
  290.2 18.0 %collective-permute-done = bf16[64,15,2,768]{3,0,2,1:T(8,128)(2,1)} collective-permute-done((bf16[64,15,2,768]{3,0,2,1:T(8,128)(2,1)}, bf16[64,15,2,768]{3,0,2,1:T(8,128)(2,1)}, u32[]{:S(2)}, u32[]{:S(2)}) %collective-permute-start) | collective-permute-done | bytes 2949152 | tf_op jit(solution)/shard_map/ppermute | solution.py:18
  315.2 18.1 %select_maximum_fusion = bf16[94,46,2,768]{3,1,0,2:T(8,128)(2,1)} fusion(bf16[64,15,2,768]{3,1,0,2:T(8,128)(2,1)S(1)} %copy.85, bf16[64,15,2,768]{3,1,0,2:T(8,128)(2,1)S(1)} %copy.84, bf16[64,16,1,768]{3,1,0,2:T(8,128)(2,1)S(1)} %bitcast.80, bf16[64,16,1,768]{3,1,0,2:T(8,128)(2,1)S(1)} %multiply_convert_fusion.1), kind=kLoop, calls=%fused_computation.60 | loop fusion | flops 99624960 | bytes 22327296 | tf_op jit(solution)/shard_map/concatenate | solution.py:16
  333.3 221.7 %while.13 = (s32[]{:T(128)}, bf16[4,16,16,768]{3,2,1,0:T(8,128)(2,1)}, s32[4]{0:T(128)S(1)}, bf16[94,46,2,768]{3,1,0,2:T(8,128)(2,1)}, bf16[64,16,6,128]{3,1,0,2...) while((s32[]{:T(128)}, ...), condition=%wide.region_10.11_spmd, body=%wide.region_5.10_spmd.sunk | while | flops 2117607168 | bytes 124344392 | solution.py:159
  334.8 5.1 constant_dynamic-slice_fusion.6
  339.9 7.7 %squeeze.25 = bf16[2116,6,128]{2,1,0:T(8,128)(2,1)} reshape(bf16[46,46,1,768]{3,1,0,2:T(8,128)(2,1)} %get-tuple-element.266) | data formatting | bytes 6500352 | tf_op jit(solution)/shard_map/while/body/eval_jaxpr/reshape;while/body/eval_jaxpr/reshape;while/body/eval_jaxpr/squeeze | solution.py:50
  350.6 9.4 %fusion.82 = (f32[6,256]{1,0:T(8,128)S(1)}, f32[6,256,2116]{1,2,0:T(8,128)}) fusion(pred[256,2116]{0,1:T(8,128)(4,1)S(1)} %fusion.81, bf16[256,6,128]{2,0,1:T(8,128)(2,1)S(1)} %bitcast.77, bf16[2116,6,128]{2,1,0:T(8,128)(2,1)} %squeeze.25), kind=kOutput, calls=%fused_computation.3.clone.1 | convolution fusion | flops 841794048 | bytes 17191936 | tf_op jit(solution)/shard_map/while/body/eval_jaxpr/qhd,khd->hqk/dot_general | solution.py:54
  363.3 7.4 %fusion.83 = f32[6,256]{1,0:T(8,128)S(1)} fusion(f32[6,256,2116]{1,2,0:T(8,128)} %get-tuple-element.267, f32[6,256]{1,0:T(8,128)S(1)} %max.13, pred[256,2116]{0,1:T(8,128)(4,1)S(1)} %fusion.81), kind=kLoop, calls=%fused_computation.4.clone.1 | loop fusion | flops 12999168 | bytes 13554688 | tf_op jit(solution)/shard_map/while/body/eval_jaxpr/reduce_sum | solution.py:68
  375.7 10.1 %fusion.85 = f32[256,6,128]{0,2,1:T(8,128)S(1)} fusion(f32[6,256,2116]{1,2,0:T(8,128)} %get-tuple-element.267, f32[6,256]{1,0:T(8,128)S(1)} %add.300, f32[6,256]{1,0:T(8,128)S(1)} %max.13, pred[256,2116]{0,1:T(8,128)(4,1)} %copy-done.4, bf16[2116,6,128]{2,1,0:T(8,128)(2,1)} %squeeze.26), kind=kOutput, calls=%fused_computation.19.clone.1 | convolution fusion | flops 848295936 | bytes 17591296 | tf_op jit(solution)/shard_map/while/body/eval_jaxpr/hqk,khd->qhd/dot_general | solution.py:73
  390.2 5.1 constant_dynamic-slice_fusion.6
  395.3 7.7 %squeeze.25 = bf16[2116,6,128]{2,1,0:T(8,128)(2,1)} reshape(bf16[46,46,1,768]{3,1,0,2:T(8,128)(2,1)} %get-tuple-element.266) | data formatting | bytes 6500352 | tf_op jit(solution)/shard_map/while/body/eval_jaxpr/reshape;while/body/eval_jaxpr/reshape;while/body/eval_jaxpr/squeeze | solution.py:50
  406.0 9.4 %fusion.82 = (f32[6,256]{1,0:T(8,128)S(1)}, f32[6,256,2116]{1,2,0:T(8,128)}) fusion(pred[256,2116]{0,1:T(8,128)(4,1)S(1)} %fusion.81, bf16[256,6,128]{2,0,1:T(8,128)(2,1)S(1)} %bitcast.77, bf16[2116,6,128]{2,1,0:T(8,128)(2,1)} %squeeze.25), kind=kOutput, calls=%fused_computation.3.clone.1 | convolution fusion | flops 841794048 | bytes 17191936 | tf_op jit(solution)/shard_map/while/body/eval_jaxpr/qhd,khd->hqk/dot_general | solution.py:54
  418.7 7.4 %fusion.83 = f32[6,256]{1,0:T(8,128)S(1)} fusion(f32[6,256,2116]{1,2,0:T(8,128)} %get-tuple-element.267, f32[6,256]{1,0:T(8,128)S(1)} %max.13, pred[256,2116]{0,1:T(8,128)(4,1)S(1)} %fusion.81), kind=kLoop, calls=%fused_computation.4.clone.1 | loop fusion | flops 12999168 | bytes 13554688 | tf_op jit(solution)/shard_map/while/body/eval_jaxpr/reduce_sum | solution.py:68
  431.1 10.1 %fusion.85 = f32[256,6,128]{0,2,1:T(8,128)S(1)} fusion(f32[6,256,2116]{1,2,0:T(8,128)} %get-tuple-element.267, f32[6,256]{1,0:T(8,128)S(1)} %add.300, f32[6,256]{1,0:T(8,128)S(1)} %max.13, pred[256,2116]{0,1:T(8,128)(4,1)} %copy-done.4, bf16[2116,6,128]{2,1,0:T(8,128)(2,1)} %squeeze.26), kind=kOutput, calls=%fused_computation.19.clone.1 | convolution fusion | flops 848295936 | bytes 17591296 | tf_op jit(solution)/shard_map/while/body/eval_jaxpr/hqk,khd->qhd/dot_general | solution.py:73
  445.6 5.1 constant_dynamic-slice_fusion.6
  450.7 7.7 %squeeze.25 = bf16[2116,6,128]{2,1,0:T(8,128)(2,1)} reshape(bf16[46,46,1,768]{3,1,0,2:T(8,128)(2,1)} %get-tuple-element.266) | data formatting | bytes 6500352 | tf_op jit(solution)/shard_map/while/body/eval_jaxpr/reshape;while/body/eval_jaxpr/reshape;while/body/eval_jaxpr/squeeze | solution.py:50
  461.4 9.4 %fusion.82 = (f32[6,256]{1,0:T(8,128)S(1)}, f32[6,256,2116]{1,2,0:T(8,128)}) fusion(pred[256,2116]{0,1:T(8,128)(4,1)S(1)} %fusion.81, bf16[256,6,128]{2,0,1:T(8,128)(2,1)S(1)} %bitcast.77, bf16[2116,6,128]{2,1,0:T(8,128)(2,1)} %squeeze.25), kind=kOutput, calls=%fused_computation.3.clone.1 | convolution fusion | flops 841794048 | bytes 17191936 | tf_op jit(solution)/shard_map/while/body/eval_jaxpr/qhd,khd->hqk/dot_general | solution.py:54
  474.1 7.4 %fusion.83 = f32[6,256]{1,0:T(8,128)S(1)} fusion(f32[6,256,2116]{1,2,0:T(8,128)} %get-tuple-element.267, f32[6,256]{1,0:T(8,128)S(1)} %max.13, pred[256,2116]{0,1:T(8,128)(4,1)S(1)} %fusion.81), kind=kLoop, calls=%fused_computation.4.clone.1 | loop fusion | flops 12999168 | bytes 13554688 | tf_op jit(solution)/shard_map/while/body/eval_jaxpr/reduce_sum | solution.py:68
  486.5 10.1 %fusion.85 = f32[256,6,128]{0,2,1:T(8,128)S(1)} fusion(f32[6,256,2116]{1,2,0:T(8,128)} %get-tuple-element.267, f32[6,256]{1,0:T(8,128)S(1)} %add.300, f32[6,256]{1,0:T(8,128)S(1)} %max.13, pred[256,2116]{0,1:T(8,128)(4,1)} %copy-done.4, bf16[2116,6,128]{2,1,0:T(8,128)(2,1)} %squeeze.26), kind=kOutput, calls=%fused_computation.19.clone.1 | convolution fusion | flops 848295936 | bytes 17591296 | tf_op jit(solution)/shard_map/while/body/eval_jaxpr/hqk,khd->qhd/dot_general | solution.py:73
  500.9 5.1 constant_dynamic-slice_fusion.6
  506.1 7.7 %squeeze.25 = bf16[2116,6,128]{2,1,0:T(8,128)(2,1)} reshape(bf16[46,46,1,768]{3,1,0,2:T(8,128)(2,1)} %get-tuple-element.266) | data formatting | bytes 6500352 | tf_op jit(solution)/shard_map/while/body/eval_jaxpr/reshape;while/body/eval_jaxpr/reshape;while/body/eval_jaxpr/squeeze | solution.py:50
  516.8 9.4 %fusion.82 = (f32[6,256]{1,0:T(8,128)S(1)}, f32[6,256,2116]{1,2,0:T(8,128)}) fusion(pred[256,2116]{0,1:T(8,128)(4,1)S(1)} %fusion.81, bf16[256,6,128]{2,0,1:T(8,128)(2,1)S(1)} %bitcast.77, bf16[2116,6,128]{2,1,0:T(8,128)(2,1)} %squeeze.25), kind=kOutput, calls=%fused_computation.3.clone.1 | convolution fusion | flops 841794048 | bytes 17191936 | tf_op jit(solution)/shard_map/while/body/eval_jaxpr/qhd,khd->hqk/dot_general | solution.py:54
  529.5 7.4 %fusion.83 = f32[6,256]{1,0:T(8,128)S(1)} fusion(f32[6,256,2116]{1,2,0:T(8,128)} %get-tuple-element.267, f32[6,256]{1,0:T(8,128)S(1)} %max.13, pred[256,2116]{0,1:T(8,128)(4,1)S(1)} %fusion.81), kind=kLoop, calls=%fused_computation.4.clone.1 | loop fusion | flops 12999168 | bytes 13554688 | tf_op jit(solution)/shard_map/while/body/eval_jaxpr/reduce_sum | solution.py:68
  541.9 10.1 %fusion.85 = f32[256,6,128]{0,2,1:T(8,128)S(1)} fusion(f32[6,256,2116]{1,2,0:T(8,128)} %get-tuple-element.267, f32[6,256]{1,0:T(8,128)S(1)} %add.300, f32[6,256]{1,0:T(8,128)S(1)} %max.13, pred[256,2116]{0,1:T(8,128)(4,1)} %copy-done.4, bf16[2116,6,128]{2,1,0:T(8,128)(2,1)} %squeeze.26), kind=kOutput, calls=%fused_computation.19.clone.1 | convolution fusion | flops 848295936 | bytes 17591296 | tf_op jit(solution)/shard_map/while/body/eval_jaxpr/hqk,khd->qhd/dot_general | solution.py:73
  555.0 10.2 %fusion.54 = f32[1024,3072]{1,0:T(8,128)} fusion(bf16[1024,768]{1,0:T(8,128)(2,1)} %bitcast.92, bf16[768,3072]{0,1:T(8,128)(2,1)} %bitcast.85), kind=kOutput, calls=%fused_computation.99 | convolution fusion | flops 4831838208 | bytes 18874368 | tf_op jit(solution)/shard_map/dot_general | solution.py:166
  566.7 117.4 %reduce-scatter.2.cloned.1.call-done = f32[1024,768]{1,0:T(8,128)} async-done(((f32[1024,3072]{1,0:T(8,128)}), f32[1024,768]{1,0:T(8,128)}) %reduce-scatter.2.cloned.1.call-update) | async-done | bytes 3145744 | tf_op jit(solution)/shard_map/reduce_scatter | solution.py:167
  (175 shorter events, 153.4 us)
Async XLA Ops:
  6.5 63.3 %copy-start = (f32[128]{0:T(128)S(1)}, f32[128]{0:T(128)}, u32[]{:S(2)}) copy-start(f32[128]{0:T(128)} %param.20) | copy-start | bytes 1540
  6.5 4.7 copy-start.8
  6.5 5.6 copy-start.6
  6.5 70.6 %all-gather.8.cloned.1.call-start = ((), (), s32[]{:S(2)}) async-start(), calls=%async_computation.4 | async-start | bytes 5308416 | tf_op jit(solution)/shard_map/all_gather | solution.py:164
  7.3 187.1 %all-gather.4.cloned.1.call-start = ((), (), s32[]{:S(2)}) async-start(), calls=%async_computation.2 | async-start | bytes 15925248 | tf_op jit(solution)/shard_map/all_gather | solution.py:121
  11.2 237.4 %all-gather.6.cloned.1.call-start = ((), (), s32[]{:S(2)}) async-start(), calls=%async_computation.3 | async-start | bytes 1769472 | tf_op jit(solution)/shard_map/all_gather | solution.py:141
  59.8 10.1 %slice-start = ((s8[6291456]{0:T(1024)(128)(4,1)}), s8[4194304]{0:T(1024)(128)(4,1)S(1)}, s32[]{:S(2)}) async-start(s8[6291456]{0:T(1024)(128)(4,1)} %bitcast.75), calls=%async_computation.6 | async-start | bytes 8388608
  61.4 8.5 %slice-start.1 = ((s8[6291456]{0:T(1024)(128)(4,1)}), s8[2097152]{0:T(1024)(128)(4,1)S(1)}, s32[]{:S(2)}) async-start(s8[6291456]{0:T(1024)(128)(4,1)} %bitcast.75), calls=%async_computation.7 | async-start | bytes 4194304
  65.2 4.6 copy-start.9
  77.2 190.9 %all-to-all-start = ((bf16[4,768,768]{2,1,0:T(8,128)(2,1)}), bf16[4,768,768]{2,1,0:T(8,128)(2,1)}, u32[]{:S(2)}, u32[]{:S(2)}) async-start(bf16[4,768,768]{2,1,0:T(8,128)(2,1)} %bitcast.84), calls=%async_computation | async-start | bytes 9437184 | tf_op jit(solution)/shard_map/all_to_all | solution.py:165
  82.2 601.9 %reduce-scatter.2.cloned.1.call-start = ((), (), s32[]{:S(2)}) async-start(), calls=%async_computation.5 | async-start | bytes 15728640 | tf_op jit(solution)/shard_map/reduce_scatter | solution.py:167
  241.9 66.3 %collective-permute-start = (bf16[64,15,2,768]{3,0,2,1:T(8,128)(2,1)}, bf16[64,15,2,768]{3,0,2,1:T(8,128)(2,1)}, u32[]{:S(2)}, u32[]{:S(2)}) collective-permute-start(bf16[64,15,2,768]{3,0,2,1:T(8,128)(2,1)} %copy.82), channel_id=1, source_target_pairs={{0,4},{4,8},{8,12},{12,16},{16,20},{20,24},{24,28},{28,0},{1,5},{5... | collective-permute-start | bytes 8847368 | tf_op jit(solution)/shard_map/ppermute | solution.py:18
  244.9 66.8 %collective-permute-start.1 = (bf16[64,15,2,768]{3,0,2,1:T(8,128)(2,1)}, bf16[64,15,2,768]{3,0,2,1:T(8,128)(2,1)}, u32[]{:S(2)}, u32[]{:S(2)}) collective-permute-start(bf16[64,15,2,768]{3,0,2,1:T(8,128)(2,1)} %copy.83), channel_id=1, source_target_pairs={{4,0},{8,4},{12,8},{16,12},{20,16},{24,20},{28,24},{0,28},{5,1},{9... | collective-permute-start | bytes 8847368 | tf_op jit(solution)/shard_map/ppermute | solution.py:20
  279.3 6.6 copy-start.10
  350.6 12.7 %copy-start.4 = (pred[256,2116]{0,1:T(8,128)(4,1)}, pred[256,2116]{0,1:T(8,128)(4,1)S(1)}, u32[]{:S(2)}) copy-start(pred[256,2116]{0,1:T(8,128)(4,1)S(1)} %fusion.81) | copy-start | bytes 1625092 | tf_op jit(solution)/shard_map/while
  350.6 9.4 %copy-start.5 = (bf16[512,6,128]{2,0,1:T(8,128)(2,1)S(1)}, bf16[512,6,128]{2,0,1:T(8,128)(2,1)}, u32[]{:S(2)}) copy-start(bf16[512,6,128]{2,0,1:T(8,128)(2,1)} %get-tuple-element.303) | copy-start | bytes 2359300 | tf_op jit(solution)/shard_map/while
  375.7 10.1 %copy-start.3 = (f32[6,256,512]{2,1,0:T(8,128)S(1)}, f32[6,256,512]{2,1,0:T(8,128)}, u32[]{:S(2)}) copy-start(f32[6,256,512]{2,1,0:T(8,128)} %copy-done.2) | copy-start | bytes 9437188 | tf_op jit(solution)/shard_map/while
  375.7 10.1 %copy-start.7 = (bf16[512,6,128]{2,0,1:T(8,128)(2,1)S(1)}, bf16[512,6,128]{2,0,1:T(8,128)(2,1)}, u32[]{:S(2)}) copy-start(bf16[512,6,128]{2,0,1:T(8,128)(2,1)} %get-tuple-element.304) | copy-start | bytes 2359300 | tf_op jit(solution)/shard_map/while
  406.0 12.7 %copy-start.4 = (pred[256,2116]{0,1:T(8,128)(4,1)}, pred[256,2116]{0,1:T(8,128)(4,1)S(1)}, u32[]{:S(2)}) copy-start(pred[256,2116]{0,1:T(8,128)(4,1)S(1)} %fusion.81) | copy-start | bytes 1625092 | tf_op jit(solution)/shard_map/while
  406.0 9.4 %copy-start.5 = (bf16[512,6,128]{2,0,1:T(8,128)(2,1)S(1)}, bf16[512,6,128]{2,0,1:T(8,128)(2,1)}, u32[]{:S(2)}) copy-start(bf16[512,6,128]{2,0,1:T(8,128)(2,1)} %get-tuple-element.303) | copy-start | bytes 2359300 | tf_op jit(solution)/shard_map/while
  431.1 10.1 %copy-start.3 = (f32[6,256,512]{2,1,0:T(8,128)S(1)}, f32[6,256,512]{2,1,0:T(8,128)}, u32[]{:S(2)}) copy-start(f32[6,256,512]{2,1,0:T(8,128)} %copy-done.2) | copy-start | bytes 9437188 | tf_op jit(solution)/shard_map/while
  431.1 10.1 %copy-start.7 = (bf16[512,6,128]{2,0,1:T(8,128)(2,1)S(1)}, bf16[512,6,128]{2,0,1:T(8,128)(2,1)}, u32[]{:S(2)}) copy-start(bf16[512,6,128]{2,0,1:T(8,128)(2,1)} %get-tuple-element.304) | copy-start | bytes 2359300 | tf_op jit(solution)/shard_map/while
  461.4 12.7 %copy-start.4 = (pred[256,2116]{0,1:T(8,128)(4,1)}, pred[256,2116]{0,1:T(8,128)(4,1)S(1)}, u32[]{:S(2)}) copy-start(pred[256,2116]{0,1:T(8,128)(4,1)S(1)} %fusion.81) | copy-start | bytes 1625092 | tf_op jit(solution)/shard_map/while
  461.4 9.4 %copy-start.5 = (bf16[512,6,128]{2,0,1:T(8,128)(2,1)S(1)}, bf16[512,6,128]{2,0,1:T(8,128)(2,1)}, u32[]{:S(2)}) copy-start(bf16[512,6,128]{2,0,1:T(8,128)(2,1)} %get-tuple-element.303) | copy-start | bytes 2359300 | tf_op jit(solution)/shard_map/while
  471.4 1.7 copy-start.2
  486.5 10.1 %copy-start.3 = (f32[6,256,512]{2,1,0:T(8,128)S(1)}, f32[6,256,512]{2,1,0:T(8,128)}, u32[]{:S(2)}) copy-start(f32[6,256,512]{2,1,0:T(8,128)} %copy-done.2) | copy-start | bytes 9437188 | tf_op jit(solution)/shard_map/while
  486.5 10.1 %copy-start.7 = (bf16[512,6,128]{2,0,1:T(8,128)(2,1)S(1)}, bf16[512,6,128]{2,0,1:T(8,128)(2,1)}, u32[]{:S(2)}) copy-start(bf16[512,6,128]{2,0,1:T(8,128)(2,1)} %get-tuple-element.304) | copy-start | bytes 2359300 | tf_op jit(solution)/shard_map/while
  516.8 12.7 %copy-start.4 = (pred[256,2116]{0,1:T(8,128)(4,1)}, pred[256,2116]{0,1:T(8,128)(4,1)S(1)}, u32[]{:S(2)}) copy-start(pred[256,2116]{0,1:T(8,128)(4,1)S(1)} %fusion.81) | copy-start | bytes 1625092 | tf_op jit(solution)/shard_map/while
  516.8 9.4 %copy-start.5 = (bf16[512,6,128]{2,0,1:T(8,128)(2,1)S(1)}, bf16[512,6,128]{2,0,1:T(8,128)(2,1)}, u32[]{:S(2)}) copy-start(bf16[512,6,128]{2,0,1:T(8,128)(2,1)} %get-tuple-element.303) | copy-start | bytes 2359300 | tf_op jit(solution)/shard_map/while
  541.9 10.1 %copy-start.3 = (f32[6,256,512]{2,1,0:T(8,128)S(1)}, f32[6,256,512]{2,1,0:T(8,128)}, u32[]{:S(2)}) copy-start(f32[6,256,512]{2,1,0:T(8,128)} %copy-done.2) | copy-start | bytes 9437188 | tf_op jit(solution)/shard_map/while
  541.9 10.1 %copy-start.7 = (bf16[512,6,128]{2,0,1:T(8,128)(2,1)S(1)}, bf16[512,6,128]{2,0,1:T(8,128)(2,1)}, u32[]{:S(2)}) copy-start(bf16[512,6,128]{2,0,1:T(8,128)(2,1)} %get-tuple-element.304) | copy-start | bytes 2359300 | tf_op jit(solution)/shard_map/while
  565.2 122.8 %copy-start.1 = (f32[128]{0:T(128)S(1)}, f32[128]{0:T(128)}, u32[]{:S(2)}) copy-start(f32[128]{0:T(128)} %param.20) | copy-start | bytes 1540
  (3 other events, 5.0 us)
Sparse Core Ops, SparseCore 0:
  9.0 55.3 all-gather.7
  66.0 128.2 all-gather.3
  196.0 23.2 all-gather.5
  565.3 118.6 reduce-scatter.1
where the time goes:
time: 704 us; the launch traced here: 695 us
  waiting for transfers between devices  248 us (35%)
  local copies, waits for them, and re-layouts  156 us (22%)
  matrix products  118 us (17%)
  other arithmetic  101 us (14%)
  blocking collectives  45.9 us (7%)
  between operations  13.6 us (2%)
  starting transfers between devices  9.2 us (1%)
    reduce_scatter x1, waiting for transfers between devices, body(): lax.psum_scatter(partial_out, 'head', scatter_dimension=1, tiled=True)  117 us
    all_gather x1, waiting for transfers between devices, body(): shard_rows = lax.all_gather(qkv_weight, 'lon', axis=0, tiled=True)  112 us
    psum x1, blocking collectives, body(): lax.psum(partial_mod, ('lon', 'head')).reshape(3, model_width)  45.9 us
    dot_general x4, matrix products, attend(): jnp.einsum('hqk,khd->qhd', image_probs, flat_values, preferred_element_ty...  40.3 us
    dot_general x4, matrix products, attend(): jnp.einsum('qhd,khd->hqk', flat_query, flat_keys, preferred_element_type=...  37.5 us
    squeeze x4, local copies, waits for them, and re-layouts, attend(): flat_keys = key_block.reshape(k_rows * k_cols, heads_here, head_dim)  30.6 us
    reduce_sum x4, other arithmetic, attend(): jnp.sum(image_exp, axis=2, keepdims=True)  29.7 us
    slice x4, local copies, waits for them, and re-layouts, one_block(): pair_block[:, :, 1]  20.5 us
  transfers between devices with their start and end apart: 7, of which 3 were waited for; matrix products, arithmetic and copies ran while one was open for 17% of the time, Pallas kernels for 0%

commit v1 on v0

--- a/solution.py
+++ b/solution.py
@@ -1,3 +1,4 @@
+import functools
 import math
 import jax
 import jax.numpy as jnp
@@ -6,6 +7,34 @@
 
 RADIUS = 15
 QROWS = 16
+
+
+def _map_tables(u_in, dim_no):
+    z = list(u_in.shape[1:])
+    z[dim_no] *= u_in.shape[0]
+    return jnp.moveaxis(u_in, 0, dim_no).reshape(z)
+
+
+def _create_modes(local_values, axis_tag):
+    world_n = lax.axis_size(axis_tag)
+    field_out = local_values[None]
+    for to_i in range(world_n.bit_length() - 1):
+        val2 = 1 << to_i
+        ledger = []
+        for jj in range(world_n):
+            ledger.append((jj, jj ^ val2))
+        raw_out = lax.ppermute(field_out, axis_tag, ledger)
+        p_next = jnp.stack([field_out, raw_out])
+        tile_out = lax.axis_index(axis_tag) >> to_i & 1
+        field_out = jnp.where(tile_out == 0, p_next, p_next[::-1]).reshape(-1, *local_values.shape)
+    return field_out
+
+
+def _view_tracks(x_local, work_x, join_dim):
+    return _map_tables(_create_modes(x_local, work_x), join_dim)
+
+
+node_recast = functools.partial(_view_tracks, work_x="lon", join_dim=0)
 
 
 def padded_2(cells, sides, width):
@@ -118,7 +147,7 @@
     local_inner = qkv_weight.shape[2]
     head_dim = q_gain.shape[0]
     local_heads = local_inner // head_dim
-    shard_rows = lax.all_gather(qkv_weight, "lon", axis=0, tiled=True)
+    shard_rows = node_recast(qkv_weight)
     row_total = shard_rows.shape[0]
     projected = jnp.dot(
         modulated,

time: 704 us -> 1080 us (1.53)
  blocking collectives: 45.9 us -> 334 us
  local copies, waits for them, and re-layouts: 156 us -> 204 us
  other arithmetic: 101 us -> 131 us
    psum x1, blocking collectives: 45.9 us -> 334 us  [body(): lax.psum(partial_mod, ('lon', 'head')).reshape(3, model_width)]
    ppermute x0 -> x3, waiting for transfers between devices: none -> 118 us  [_create_modes(): raw_out = lax.ppermute(field_out, axis_tag, ledger)]
    all_gather x1 -> x0, waiting for transfers between devices: 112 us -> none  [body(): shard_rows = lax.all_gather(qkv_weight, 'lon', axis=0, tiled=True)]
    another operation x0 -> x2, local copies, waits for them, and re-layouts: none -> 37.4 us  [the longest x1 23.4 us: body(): shard_rows.reshape(row_total, 3 * local_inner)]
    another operation x0 -> x4, other arithmetic: none -> 18.4 us  [_create_modes(): p_next = jnp.stack([field_out, raw_out])]
    reshape x0 -> x1, local copies, waits for them, and re-layouts: none -> 14.1 us  [_create_modes(): jnp.where(tile_out == 0, p_next, p_next[::-1])]
    select_n x0 -> x2, other arithmetic: none -> 13.1 us  [_create_modes(): jnp.where(tile_out == 0, p_next, p_next[::-1])]
  transfers between devices with their start and end apart: 7 -> 9, of which waited for: 3 -> 4; matrix products, arithmetic and copies ran while one was open for 17% -> 19% of each run, Pallas kernels for 0% -> 0%
where the time goes in v1:
time: 1080 us; the launch traced here: 1070 us
  blocking collectives  334 us (31%)
  waiting for transfers between devices  254 us (24%)
  local copies, waits for them, and re-layouts  204 us (19%)
  other arithmetic  131 us (12%)
  matrix products  118 us (11%)
  starting transfers between devices  15.4 us (1%)
  between operations  13.6 us (1%)
    psum x1, blocking collectives, body(): lax.psum(partial_mod, ('lon', 'head')).reshape(3, model_width)  334 us
    ppermute x3, waiting for transfers between devices, _create_modes(): raw_out = lax.ppermute(field_out, axis_tag, ledger)  118 us
    reduce_scatter x1, waiting for transfers between devices, body(): lax.psum_scatter(partial_out, 'head', scatter_dimension=1, tiled=True)  118 us
    dot_general x4, matrix products, attend(): jnp.einsum('hqk,khd->qhd', image_probs, flat_values, preferred_element_ty...  40.1 us
    dot_general x4, matrix products, attend(): jnp.einsum('qhd,khd->hqk', flat_query, flat_keys, preferred_element_type=...  37.5 us
    squeeze x4, local copies, waits for them, and re-layouts, attend(): flat_keys = key_block.reshape(k_rows * k_cols, heads_here, head_dim)  30.6 us
    reduce_sum x4, other arithmetic, attend(): jnp.sum(image_exp, axis=2, keepdims=True)  29.7 us
    another operation x1, local copies, waits for them, and re-layouts, body(): shard_rows.reshape(row_total, 3 * local_inner)  23.4 us
  transfers between devices with their start and end apart: 9, of which 4 were waited for; matrix products, arithmetic and copies ran while one was open for 19% of the time, Pallas kernels for 0%

profile of v1, /device:TPU:0, one launch (start us, length us, event | category | flops | bytes accessed | tf_op | source)
XLA Modules:
  0.0 1074.7 jit_solution(6133735337892858861)
XLA Ops:
  17.9 115.1 %collective-permute-done.1 = bf16[2,384,3,768]{3,1,2,0:T(8,128)(2,1)} collective-permute-done((bf16[2,384,3,768]{3,1,2,0:T(8,128)(2,1)}, bf16[2,384,3,768]{3,1,2,0:T(8,128)(2,1)}, u32[]{:S(2)}, u32[]{:S(2)}) %collective-permute-start.1) | collective-permute-done | bytes 3538976 | tf_op jit(solution)/shard_map/ppermute | solution.py:26
  139.9 14.1 %copy.83 = bf16[4,384,3,768]{1,0,3,2:T(4,128)(2,1)} copy(bf16[4,384,3,768]{3,1,2,0:T(8,128)(2,1)} %bitcast.85) | data formatting | bytes 14155776 | tf_op jit(solution)/shard_map/reshape | solution.py:29
  161.6 334.1 %psum.7 = f32[3,3072]{1,0:T(4,128)S(1)} all-reduce(f32[3,3072]{1,0:T(4,128)S(1)} %reshape.299), channel_id=1, replica_groups=mesh['lon'=8,'head'=4] {'lon','head'}, use_global_device_ids=true, to_apply=%region_0.1 | all-reduce | flops 9216 | bytes 73728 | tf_op jit(solution)/shard_map/psum | solution.py:137
  504.8 6.5 fusion.38
  511.4 13.9 %copy.84 = bf16[1,4,384,3,768]{2,1,0,4,3:T(4,128)(2,1)} copy(bf16[1,4,384,3,768]{4,2,3,1,0:T(8,128)(2,1)} %bitcast.86) | data formatting | bytes 14155776 | tf_op jit(solution)/shard_map/stack;reshape | solution.py:27
  530.5 11.2 %pad_maximum_fusion = bf16[2,4,384,3,768]{2,1,0,4,3:T(4,128)(2,1)S(1)} fusion(bf16[1,4,384,3,768]{2,1,0,4,3:T(4,128)(2,1)} %bitcast.19, bf16[1,4,384,3,768]{2,1,0,4,3:T(4,128)(2,1)} %copy.84), kind=kLoop, calls=%fused_computation.59 | loop fusion | flops 7077888 | bytes 28311552 | tf_op jit(solution)/shard_map/stack | solution.py:27
  541.8 8.8 reverse_select_fusion
  550.6 23.4 %reshape_reshape_reshape.3 = bf16[3072,2304]{0,1:T(8,128)(2,1)} reshape(bf16[2,4,384,3,768]{2,1,0,4,3:T(4,128)(2,1)} %reverse_select_fusion) | data formatting | bytes 28311552 | tf_op jit(solution)/shard_map/reshape;reshape;reshape | solution.py:154
  574.1 19.7 %broadcast_add_fusion.1 = f32[1024,3,768]{2,0,1:T(8,128)S(1)} fusion(f32[3,768]{1,0:T(4,128)S(1)} %convert_element_type.84, bf16[1024,3072,1]{1,0,2:T(8,128)(2,1)} %bitcast.94, bf16[3,768,3072]{2,1,0:T(8,128)(2,1)} %bitcast.91), kind=kOutput, calls=%fused_computation.72 | convolution fusion | flops 14497873920 | bytes 29893632 | tf_op jit(solution)/shard_map/dot_general | solution.py:152
  628.3 5.6 fusion.50
  647.8 6.6 copy.99
  669.9 17.9 %collective-permute-done.3 = bf16[64,15,2,768]{3,0,2,1:T(8,128)(2,1)} collective-permute-done((bf16[64,15,2,768]{3,0,2,1:T(8,128)(2,1)}, bf16[64,15,2,768]{3,0,2,1:T(8,128)(2,1)}, u32[]{:S(2)}, u32[]{:S(2)}) %collective-permute-start.3) | collective-permute-done | bytes 2949152 | tf_op jit(solution)/shard_map/ppermute | solution.py:47
  694.8 18.1 %select_maximum_fusion = bf16[94,46,2,768]{3,1,0,2:T(8,128)(2,1)} fusion(bf16[64,15,2,768]{3,1,0,2:T(8,128)(2,1)S(1)} %copy.90, bf16[64,15,2,768]{3,1,0,2:T(8,128)(2,1)S(1)} %copy.89, bf16[64,16,1,768]{3,1,0,2:T(8,128)(2,1)S(1)} %bitcast.90, bf16[64,16,1,768]{3,1,0,2:T(8,128)(2,1)S(1)} %multiply_convert_fusion.1), kind=kLoop, calls=%fused_computation.60 | loop fusion | flops 99624960 | bytes 22327296 | tf_op jit(solution)/shard_map/concatenate | solution.py:45
  712.9 221.5 %while.13 = (s32[]{:T(128)}, bf16[4,16,16,768]{3,2,1,0:T(8,128)(2,1)}, s32[4]{0:T(128)S(1)}, bf16[94,46,2,768]{3,1,0,2:T(8,128)(2,1)}, bf16[64,16,6,128]{3,1,0,2...) while((s32[]{:T(128)}, ...), condition=%wide.region_10.11_spmd, body=%wide.region_5.10_spmd.sunk | while | flops 2117607168 | bytes 124344392 | solution.py:188
  719.5 7.7 squeeze.25
  730.2 9.4 fusion.81
  742.9 7.4 fusion.82
  755.3 10.0 fusion.84
  774.9 7.7 squeeze.25
  785.6 9.4 fusion.81
  798.3 7.4 fusion.82
  810.6 10.0 fusion.84
  830.2 7.7 squeeze.25
  840.9 9.4 fusion.81
  853.6 7.4 fusion.82
  866.0 10.0 fusion.84
  885.5 7.7 squeeze.25
  896.3 9.4 fusion.81
  908.9 7.4 fusion.82
  921.3 10.0 fusion.84
  934.4 10.1 fusion.52
  946.0 118.0 %reduce-scatter.2.cloned.1.call-done = f32[1024,768]{1,0:T(8,128)} async-done(((f32[1024,3072]{1,0:T(8,128)}), f32[1024,768]{1,0:T(8,128)}) %reduce-scatter.2.cloned.1.call-update) | async-done | bytes 3145744 | tf_op jit(solution)/shard_map/reduce_scatter | solution.py:196
  (188 shorter events, 196.5 us)
Async XLA Ops:
  6.5 489.1 %copy-start = (f32[128]{0:T(128)S(1)}, f32[128]{0:T(128)}, u32[]{:S(2)}) copy-start(f32[128]{0:T(128)} %param.20) | copy-start | bytes 1540
  6.5 518.7 %all-gather.5.cloned.1.call-start = ((), (), s32[]{:S(2)}) async-start(), calls=%async_computation.3 | async-start | bytes 5308416 | tf_op jit(solution)/shard_map/all_gather | solution.py:193
  6.5 4.0 collective-permute-start
  7.3 621.0 %all-gather.3.cloned.1.call-start = ((), (), s32[]{:S(2)}) async-start(), calls=%async_computation.2 | async-start | bytes 1769472 | tf_op jit(solution)/shard_map/all_gather | solution.py:170
  15.0 118.0 %collective-permute-start.1 = (bf16[2,384,3,768]{3,1,2,0:T(8,128)(2,1)}, bf16[2,384,3,768]{3,1,2,0:T(8,128)(2,1)}, u32[]{:S(2)}, u32[]{:S(2)}) collective-permute-start(bf16[2,384,3,768]{3,1,2,0:T(8,128)(2,1)} %get-tuple-element.203), channel_id=1, source_target_pairs={{0,8},{4,12},{8,0},{12,4},{16,24},{20,28},{24,16},{28,20},{1,9},{5... | collective-permute-start | bytes 10616840 | tf_op jit(solution)/shard_map/ppermute | solution.py:26
  139.9 16.8 %copy-start.8 = (bf16[2,64,768]{2,1,0:T(8,128)(2,1)S(1)}, bf16[2,64,768]{2,1,0:T(8,128)(2,1)}, u32[]{:S(2)}) copy-start(bf16[2,64,768]{2,1,0:T(8,128)(2,1)} %param.21) | copy-start | bytes 589828
  139.9 17.8 %copy-start.6 = (bf16[96,3,3072]{2,0,1:T(8,128)(2,1)S(1)}, bf16[96,3,3072]{2,0,1:T(8,128)(2,1)}, u32[]{:S(2)}) copy-start(bf16[96,3,3072]{2,0,1:T(8,128)(2,1)} %param.15) | copy-start | bytes 5308420
  154.0 7.6 copy-start.10
  154.0 376.5 %collective-permute-start.2 = (bf16[4,384,3,768]{1,0,3,2:T(4,128)(2,1)}, bf16[4,384,3,768]{1,0,3,2:T(4,128)(2,1)}, u32[]{:S(2)}, u32[]{:S(2)}) collective-permute-start(bf16[4,384,3,768]{1,0,3,2:T(4,128)(2,1)} %copy.83), channel_id=1, source_target_pairs={{0,16},{4,20},{8,24},{12,28},{16,0},{20,4},{24,8},{28,12},{1,17},{... | collective-permute-start | bytes 21233672 | tf_op jit(solution)/shard_map/ppermute | solution.py:26
  159.0 345.8 %slice-start = ((s8[6291456]{0:T(1024)(128)(4,1)}), s8[2097152]{0:T(1024)(128)(4,1)S(1)}, s32[]{:S(2)}) async-start(s8[6291456]{0:T(1024)(128)(4,1)} %bitcast.83), calls=%async_computation.5 | async-start | bytes 4194304
  495.7 9.1 slice-start.1
  525.3 122.5 %all-to-all-start = ((bf16[4,768,768]{2,1,0:T(8,128)(2,1)}), bf16[4,768,768]{2,1,0:T(8,128)(2,1)}, u32[]{:S(2)}, u32[]{:S(2)}) async-start(bf16[4,768,768]{2,1,0:T(8,128)(2,1)} %bitcast.95), calls=%async_computation | async-start | bytes 9437184 | tf_op jit(solution)/shard_map/all_to_all | solution.py:194
  530.3 533.8 %reduce-scatter.2.cloned.1.call-start = ((), (), s32[]{:S(2)}) async-start(), calls=%async_computation.4 | async-start | bytes 15728640 | tf_op jit(solution)/shard_map/reduce_scatter | solution.py:196
  621.7 66.2 %collective-permute-start.3 = (bf16[64,15,2,768]{3,0,2,1:T(8,128)(2,1)}, bf16[64,15,2,768]{3,0,2,1:T(8,128)(2,1)}, u32[]{:S(2)}, u32[]{:S(2)}) collective-permute-start(bf16[64,15,2,768]{3,0,2,1:T(8,128)(2,1)} %copy.87), channel_id=1, source_target_pairs={{0,4},{4,8},{8,12},{12,16},{16,20},{20,24},{24,28},{28,0},{1,5},{5... | collective-permute-start | bytes 8847368 | tf_op jit(solution)/shard_map/ppermute | solution.py:47
  624.7 66.5 %collective-permute-start.4 = (bf16[64,15,2,768]{3,0,2,1:T(8,128)(2,1)}, bf16[64,15,2,768]{3,0,2,1:T(8,128)(2,1)}, u32[]{:S(2)}, u32[]{:S(2)}) collective-permute-start(bf16[64,15,2,768]{3,0,2,1:T(8,128)(2,1)} %copy.88), channel_id=1, source_target_pairs={{4,0},{8,4},{12,8},{16,12},{20,16},{24,20},{28,24},{0,28},{5,1},{9... | collective-permute-start | bytes 8847368 | tf_op jit(solution)/shard_map/ppermute | solution.py:49
  730.2 12.7 %copy-start.4 = (pred[256,2116]{0,1:T(8,128)(4,1)}, pred[256,2116]{0,1:T(8,128)(4,1)S(1)}, u32[]{:S(2)}) copy-start(pred[256,2116]{0,1:T(8,128)(4,1)S(1)} %fusion.80) | copy-start | bytes 1625092 | tf_op jit(solution)/shard_map/while
  730.2 9.4 copy-start.5
  755.3 10.0 copy-start.3
  755.3 10.1 copy-start.7
  785.6 12.7 %copy-start.4 = (pred[256,2116]{0,1:T(8,128)(4,1)}, pred[256,2116]{0,1:T(8,128)(4,1)S(1)}, u32[]{:S(2)}) copy-start(pred[256,2116]{0,1:T(8,128)(4,1)S(1)} %fusion.80) | copy-start | bytes 1625092 | tf_op jit(solution)/shard_map/while
  785.6 9.4 copy-start.5
  810.6 10.0 copy-start.3
  810.6 10.1 copy-start.7
  840.9 12.7 %copy-start.4 = (pred[256,2116]{0,1:T(8,128)(4,1)}, pred[256,2116]{0,1:T(8,128)(4,1)S(1)}, u32[]{:S(2)}) copy-start(pred[256,2116]{0,1:T(8,128)(4,1)S(1)} %fusion.80) | copy-start | bytes 1625092 | tf_op jit(solution)/shard_map/while
  840.9 9.4 copy-start.5
  866.0 10.0 copy-start.3
  866.0 10.1 copy-start.7
  896.2 12.7 %copy-start.4 = (pred[256,2116]{0,1:T(8,128)(4,1)}, pred[256,2116]{0,1:T(8,128)(4,1)S(1)}, u32[]{:S(2)}) copy-start(pred[256,2116]{0,1:T(8,128)(4,1)S(1)} %fusion.80) | copy-start | bytes 1625092 | tf_op jit(solution)/shard_map/while
  896.3 9.4 copy-start.5
  921.3 10.0 copy-start.3
  921.3 10.1 copy-start.7
  944.5 123.5 %copy-start.1 = (f32[128]{0:T(128)S(1)}, f32[128]{0:T(128)}, u32[]{:S(2)}) copy-start(f32[128]{0:T(128)} %param.20) | copy-start | bytes 1540
  (6 other events, 17.8 us)
Sparse Core Ops, SparseCore 0:
  9.0 86.8 all-gather.4
  157.8 172.8 all-gather.2
  944.7 119.3 reduce-scatter.1
